TPU v7x, 512 devices: a whole 4x4x16 slice. The times are simulated.
512 devices in a mesh: dp: 32 (over z, y_hi), expert: 16 (over y_lo, x, core).
Axes of the slice: x: 4, y: 4 (y_hi: 2, y_lo: 2; y = y_hi * 2 + y_lo), z: 16, core: 2. Of those that a mesh axis runs over, the one named last changes fastest.
Arguments:
- weight: bfloat16 [16, 1024, 4096], P('expert', None, 'dp'), may hold values from -0.1875 to 0.1875
- first_moment: float32 [16, 1024, 4096], P('expert', None, 'dp'), may hold values from -3 to 3
- second_moment: float32 [16, 1024, 4096], P('expert', None, 'dp'), may hold values from 0.01 to 1
- gate_act: bfloat16 [16, 4096, 1024], P('expert', 'dp'), may hold values from -6 to 6
- up_act: bfloat16 [16, 4096, 1024], P('expert', 'dp'), may hold values from -6 to 6
- out_grad: bfloat16 [16, 4096, 4096], P('expert', 'dp'), may hold values from -0.29882812 to 0.29882812
- old_host: int32 [16], replicated, may hold values from 0 to 15, each once
- new_host: int32 [16], replicated, may hold values from 0 to 15, each once
- counts: int32 [32, 16], replicated, may hold values from 1 to 128, as said below
Outputs:
- expert_out: bfloat16 [16, 4096, 4096], P('expert', 'dp')
- new_weight: bfloat16 [16, 1024, 4096], P('expert', None, 'dp')
- new_first: float32 [16, 1024, 4096], P('expert', None, 'dp')
- new_second: float32 [16, 1024, 4096], P('expert', None, 'dp')
Inputs may be any that keep to these rules, and one draw needn't show every extreme that they name: `old_host`: each expert's host index appears once. `new_host`: each expert's host index appears once. `counts`: some expert from some replica fills all 128 slots.
All inputs are finite; a program needn't handle non-finite values.
Results may differ from a plain program's by a relative error of at most 0.0049.
Values may be sent and summed in bfloat16 or wider, within the bound.
No kernel may reach another device: no remote copies, remote signals or barrier semaphores. Data moves between devices by JAX's collectives and lax.ppermute only.
A program may use at most 64 MiB of HBM per device.

v0:
```python
import jax
import jax.numpy as jnp
from jax import lax
from jax.sharding import PartitionSpec as P

beta_one = 0.9
beta_two = 0.999
learning_rate = 0.001
epsilon_value = 1e-08
bias_one = 0.9999734386011124
bias_two = 0.0952078528863


def local(
    weight, first_moment, second_moment, gate_act, up_act, out_grad, old_host, new_host, counts
):
    host_count = lax.axis_size("expert")
    my_host = lax.axis_index("expert")
    my_replica = lax.axis_index("dp")
    expert_ids = jnp.arange(new_host.shape[0], dtype=jnp.int32)
    host_ids = jnp.arange(host_count, dtype=jnp.int32)
    matches = new_host[None, :] == host_ids[:, None]
    source_of = jnp.sum(jnp.where(matches, old_host[None, :], 0), axis=1)
    expert_of = jnp.sum(jnp.where(matches, expert_ids[None, :], 0), axis=1)
    my_expert = expert_of[my_host]
    my_source = source_of[my_host]
    hidden_units = weight.shape[1]
    columns = weight.shape[2]
    block_rows = hidden_units // host_count

    def reorder(received):
        return received.reshape(host_count, block_rows, columns)[source_of].reshape(
            hidden_units, columns
        )

    shards = lax.all_gather(weight, "expert", axis=0, tiled=True)
    picked = jnp.arange(shards.shape[0], dtype=jnp.int32) == my_source
    moved_weight = jnp.sum(jnp.where(picked[:, None, None], shards, jnp.zeros_like(shards)), axis=0)
    spread_first, spread_second = (
        lax.all_to_all(first_moment[0], "expert", split_axis=0, concat_axis=0, tiled=True),
        lax.all_to_all(second_moment[0], "expert", split_axis=0, concat_axis=0, tiled=True),
    )
    moved_first, moved_second = (
        lax.all_to_all(reorder(spread_first), "expert", split_axis=0, concat_axis=0, tiled=True),
        lax.all_to_all(reorder(spread_second), "expert", split_axis=0, concat_axis=0, tiled=True),
    )
    live_rows = counts[:, my_expert]
    slot_ids = jnp.arange(gate_act.shape[1], dtype=jnp.int32)
    filled = slot_ids < live_rows[my_replica]
    activated = jax.nn.silu(gate_act[0].astype(jnp.float32)) * up_act[0].astype(jnp.float32)
    hidden = jnp.where(filled[:, None], activated, jnp.float32(0.0)).astype(jnp.bfloat16)
    grad_columns = lax.all_to_all(out_grad[0], "dp", split_axis=1, concat_axis=0, tiled=True)
    shards = lax.all_gather(hidden, "dp", axis=0, tiled=True)
    grad_sum = jnp.einsum("rf,rc->fc", shards, grad_columns, preferred_element_type=jnp.float32)
    produced = jnp.dot(shards, moved_weight, preferred_element_type=jnp.float32).astype(
        jnp.bfloat16
    )
    output_columns = produced
    grad_sum, output_columns = (grad_sum, output_columns)
    output = lax.all_to_all(output_columns, "dp", split_axis=0, concat_axis=1, tiled=True)
    new_first = beta_one * moved_first + (1.0 - beta_one) * grad_sum
    new_second = beta_two * moved_second + (1.0 - beta_two) * grad_sum * grad_sum
    update = (
        learning_rate * (new_first / bias_one) / (jnp.sqrt(new_second / bias_two) + epsilon_value)
    )
    new_weight = (moved_weight.astype(jnp.float32) - update).astype(jnp.bfloat16)
    return (output[None], new_weight[None], new_first[None], new_second[None])


def solution(mesh):
    return jax.shard_map(
        local,
        mesh=mesh,
        in_specs=(
            P("expert", None, "dp"),
            P("expert", None, "dp"),
            P("expert", None, "dp"),
            P("expert", "dp", None),
            P("expert", "dp", None),
            P("expert", "dp", None),
            P(),
            P(),
            P(),
        ),
        out_specs=(
            P("expert", "dp", None),
            P("expert", None, "dp"),
            P("expert", None, "dp"),
            P("expert", None, "dp"),
        ),
        check_vma=False,
    )
```

profile of v0, /device:TPU:2, one launch (start us, length us, event | category | flops | bytes accessed | tf_op | source)
XLA Modules:
  0.0 364.8 jit_solution(6703636606916573695)
XLA Ops:
  7.2 0.7 all-gather.5.cloned.1.call-update
  7.9 0.8 select_reduce_fusion.1
  11.3 1.3 dynamic_slice.11
  13.2 1.9 fusion.6
  15.2 17.0 %all_to_all.65 = f32[16,64,128]{2,1,0:T(8,128)S(1)} all-to-all(f32[16,64,128]{2,1,0:T(8,128)} %bitcast.38), channel_id=1, replica_groups=mesh['dp'=32,'expert'=16] {'expert'}, dimensions={0} | all-to-all | bytes 1048576 | tf_op jit(solution)/shard_map/all_to_all | solution.py:41
  32.2 6.7 %all-to-all-start.1 = ((f32[16,64,128]{2,1,0:T(8,128)}), f32[16,64,128]{2,1,0:T(8,128)S(1)}, u32[]{:S(2)}, u32[]{:S(2)}) async-start(f32[16,64,128]{2,1,0:T(8,128)} %bitcast.39), calls=%async_computation.1 | async-start | bytes 1048576 | tf_op jit(solution)/shard_map/all_to_all | solution.py:40
  38.9 1.4 gather_fusion.1
  40.2 10.6 %all-to-all-done.1 = f32[16,64,128]{2,1,0:T(8,128)S(1)} async-done(((f32[16,64,128]{2,1,0:T(8,128)}), f32[16,64,128]{2,1,0:T(8,128)S(1)}, u32[]{:S(2)}, u32[]{:S(2)}) %all-to-all-start.1) | async-done | bytes 524320 | tf_op jit(solution)/shard_map/all_to_all | solution.py:40
  50.8 6.4 %all-to-all-start.5 = ((f32[16,64,128]{2,1,0:T(8,128)}), f32[16,64,128]{2,1,0:T(8,128)S(1)}, u32[]{:S(2)}, u32[]{:S(2)}) async-start(f32[16,64,128]{2,1,0:T(8,128)} %gather_fusion.1), calls=%async_computation.5 | async-start | bytes 1048576 | tf_op jit(solution)/shard_map/all_to_all | solution.py:45
  57.2 1.4 gather_fusion
  58.6 7.7 %all-to-all-done.5 = f32[16,64,128]{2,1,0:T(8,128)S(1)} async-done(((f32[16,64,128]{2,1,0:T(8,128)}), f32[16,64,128]{2,1,0:T(8,128)S(1)}, u32[]{:S(2)}, u32[]{:S(2)}) %all-to-all-start.5) | async-done | bytes 524320 | tf_op jit(solution)/shard_map/all_to_all | solution.py:45
  66.3 5.5 %all-to-all-start.2 = ((f32[16,64,128]{2,1,0:T(8,128)}), f32[16,64,128]{2,1,0:T(8,128)S(1)}, u32[]{:S(2)}, u32[]{:S(2)}) async-start(f32[16,64,128]{2,1,0:T(8,128)} %gather_fusion), calls=%async_computation.2 | async-start | bytes 1048576 | tf_op jit(solution)/shard_map/all_to_all | solution.py:44
  71.8 2.3 copy.22
  74.1 5.4 %all-to-all-done.2 = f32[16,64,128]{2,1,0:T(8,128)S(1)} async-done(((f32[16,64,128]{2,1,0:T(8,128)}), f32[16,64,128]{2,1,0:T(8,128)S(1)}, u32[]{:S(2)}, u32[]{:S(2)}) %all-to-all-start.2) | async-done | bytes 524320 | tf_op jit(solution)/shard_map/all_to_all | solution.py:44
  79.5 14.5 %all-to-all-start.3 = ((bf16[128,32,128]{0,2,1:T(8,128)(2,1)}), bf16[128,32,128]{0,2,1:T(8,128)(2,1)S(1)}, u32[]{:S(2)}, u32[]{:S(2)}) async-start(bf16[128,32,128]{0,2,1:T(8,128)(2,1)} %bitcast.12), calls=%async_computation.3 | async-start | bytes 2097152 | tf_op jit(solution)/shard_map/all_to_all | solution.py:52
  95.3 3.1 select_reduce_fusion
  98.4 196.5 %all-gather.3.cloned.1.call-done = bf16[4096,1024]{1,0:T(8,128)(2,1)} async-done(((bf16[128,1024]{1,0:T(8,128)(2,1)}), bf16[4096,1024]{1,0:T(8,128)(2,1)}) %all-gather.3.cloned.1.call-update) | async-done | bytes 8388624 | tf_op jit(solution)/shard_map/all_gather | solution.py:53
  294.9 6.7 %convolution_convert_fusion = bf16[4096,128]{1,0:T(8,128)(2,1)} fusion(bf16[4096,1024]{1,0:T(8,128)(2,1)} %all-gather.3.cloned.1.call-done, bf16[1024,128]{1,0:T(8,128)(2,1)S(1)} %select_reduce_fusion), kind=kOutput, calls=%fused_computation.2 | convolution fusion | flops 1074266112 | bytes 9699328 | tf_op jit(solution)/shard_map/dot_general | solution.py:55
  301.6 7.6 %all-to-all-start = ((bf16[32,128,128]{2,1,0:T(8,128)(2,1)}), bf16[32,128,128]{2,1,0:T(8,128)(2,1)S(1)}, u32[]{:S(2)}, u32[]{:S(2)}) async-start(bf16[32,128,128]{2,1,0:T(8,128)(2,1)} %bitcast.36), calls=%async_computation | async-start | bytes 2097152 | tf_op jit(solution)/shard_map/all_to_all | solution.py:60
  309.2 0.9 broadcast_multiply_fusion
  310.0 0.9 broadcast_multiply_fusion.1
  311.6 7.1 %fusion.7 = (bf16[1,1024,128]{2,1,0:T(8,128)(2,1)}, f32[1024,128]{1,0:T(8,128)}, f32[1024,128]{1,0:T(8,128)}) fusion(bf16[1024,128]{1,0:T(8,128)(2,1)S(1)} %select_reduce_fusion, f32[16,64,128]{2,1,0:T(8,128)} %broadcast_multiply_fusion.1, f32[16,64,128]{2,1,0:T(8,128)} %broadcast_multiply_fusion, bf16[4096,1024]{1,0:T(8,128)(2,1)} %all-gather.3.cloned.1.call-done, ...), kind=kOutput, calls=%fused_computation.18 | convolution fusion | flops 1075314688 | bytes 12058624 | tf_op jit(solution)/shard_map/rf,rc->fc/dot_general | solution.py:54
  318.8 37.2 %all-to-all-done = bf16[32,128,128]{2,1,0:T(8,128)(2,1)S(1)} async-done(((bf16[32,128,128]{2,1,0:T(8,128)(2,1)}), bf16[32,128,128]{2,1,0:T(8,128)(2,1)S(1)}, u32[]{:S(2)}, u32[]{:S(2)}) %all-to-all-start) | async-done | bytes 1048608 | tf_op jit(solution)/shard_map/all_to_all | solution.py:60
  356.7 1.3 broadcast_in_dim.68
  (13 shorter events, 3.9 us)
Async XLA Ops:
  7.2 88.1 %all-gather.5.cloned.1.call-start = ((), (), s32[]{:S(2)}) async-start(), calls=%async_computation.7 | async-start | bytes 4456448 | tf_op jit(solution)/shard_map/all_gather | solution.py:36
  7.9 287.0 %all-gather.3.cloned.1.call-start = ((), (), s32[]{:S(2)}) async-start(), calls=%async_computation.6 | async-start | bytes 8650752 | tf_op jit(solution)/shard_map/all_gather | solution.py:53
  32.2 18.6 %all-to-all-start.1 = ((f32[16,64,128]{2,1,0:T(8,128)}), f32[16,64,128]{2,1,0:T(8,128)S(1)}, u32[]{:S(2)}, u32[]{:S(2)}) async-start(f32[16,64,128]{2,1,0:T(8,128)} %bitcast.39), calls=%async_computation.1 | async-start | bytes 1048576 | tf_op jit(solution)/shard_map/all_to_all | solution.py:40
  50.8 15.5 %all-to-all-start.5 = ((f32[16,64,128]{2,1,0:T(8,128)}), f32[16,64,128]{2,1,0:T(8,128)S(1)}, u32[]{:S(2)}, u32[]{:S(2)}) async-start(f32[16,64,128]{2,1,0:T(8,128)} %gather_fusion.1), calls=%async_computation.5 | async-start | bytes 1048576 | tf_op jit(solution)/shard_map/all_to_all | solution.py:45
  66.3 13.2 %all-to-all-start.2 = ((f32[16,64,128]{2,1,0:T(8,128)}), f32[16,64,128]{2,1,0:T(8,128)S(1)}, u32[]{:S(2)}, u32[]{:S(2)}) async-start(f32[16,64,128]{2,1,0:T(8,128)} %gather_fusion), calls=%async_computation.2 | async-start | bytes 1048576 | tf_op jit(solution)/shard_map/all_to_all | solution.py:44
  79.5 222.0 %all-to-all-start.3 = ((bf16[128,32,128]{0,2,1:T(8,128)(2,1)}), bf16[128,32,128]{0,2,1:T(8,128)(2,1)S(1)}, u32[]{:S(2)}, u32[]{:S(2)}) async-start(bf16[128,32,128]{0,2,1:T(8,128)(2,1)} %bitcast.12), calls=%async_computation.3 | async-start | bytes 2097152 | tf_op jit(solution)/shard_map/all_to_all | solution.py:52
  301.6 54.4 %all-to-all-start = ((bf16[32,128,128]{2,1,0:T(8,128)(2,1)}), bf16[32,128,128]{2,1,0:T(8,128)(2,1)S(1)}, u32[]{:S(2)}, u32[]{:S(2)}) async-start(bf16[32,128,128]{2,1,0:T(8,128)(2,1)} %bitcast.36), calls=%async_computation | async-start | bytes 2097152 | tf_op jit(solution)/shard_map/all_to_all | solution.py:60
Sparse Core Ops, SparseCore 0:
  10.1 57.1 all-gather.4
  71.0 223.7 all-gather.2
where the time goes:
time: 366 us; the launch traced here: 365 us
  waiting for transfers between devices  258 us (70%)
  starting transfers between devices  40.7 us (11%)
  blocking collectives  17 us (5%)
  between operations  16.1 us (4%)
  matrix products  13.8 us (4%)
  local copies, waits for them, and re-layouts  10.1 us (3%)
  other arithmetic  8.89 us (2%)
    all_gather x1, waiting for transfers between devices, local(): shards = lax.all_gather(hidden, 'dp', axis=0, tiled=True)  196 us
    all_to_all x1, waiting for transfers between devices, local(): lax.all_to_all(output_columns, 'dp', split_axis=0, concat_axis=1, tiled=T...  37.2 us
    all_to_all x1, blocking collectives, local(): lax.all_to_all(second_moment[0], 'expert', split_axis=0, concat_axis=0, t...  17 us
    all_to_all x1, starting transfers between devices, local(): lax.all_to_all(out_grad[0], 'dp', split_axis=1, concat_axis=0, tiled=True)  14.5 us
    all_to_all x1, waiting for transfers between devices, local(): lax.all_to_all(first_moment[0], 'expert', split_axis=0, concat_axis=0, ti...  10.6 us
    all_to_all x1, waiting for transfers between devices, local(): lax.all_to_all(reorder(spread_second), 'expert', split_axis=0, concat_axi...  7.74 us
    all_to_all x1, starting transfers between devices, local(): lax.all_to_all(output_columns, 'dp', split_axis=0, concat_axis=1, tiled=T...  7.6 us
  transfers between devices with their start and end apart: 7, of which 5 were waited for; matrix products, arithmetic and copies ran while one was open for 8% of the time, Pallas kernels for 0%

commit v1 on v0

--- a/solution.py
+++ b/solution.py
@@ -9,6 +9,13 @@
 epsilon_value = 1e-08
 bias_one = 0.9999734386011124
 bias_two = 0.0952078528863
+
+
+def exchange_gather(x, axis, d):
+    size = lax.axis_size(axis)
+    blocks = jnp.stack([x for _ in range(size)])
+    blocks = lax.all_to_all(blocks, axis, split_axis=0, concat_axis=0)
+    return jnp.concatenate(blocks, axis=d)
 
 
 def local(
@@ -50,7 +57,7 @@
     activated = jax.nn.silu(gate_act[0].astype(jnp.float32)) * up_act[0].astype(jnp.float32)
     hidden = jnp.where(filled[:, None], activated, jnp.float32(0.0)).astype(jnp.bfloat16)
     grad_columns = lax.all_to_all(out_grad[0], "dp", split_axis=1, concat_axis=0, tiled=True)
-    shards = lax.all_gather(hidden, "dp", axis=0, tiled=True)
+    shards = exchange_gather(hidden, "dp", 0)
     grad_sum = jnp.einsum("rf,rc->fc", shards, grad_columns, preferred_element_type=jnp.float32)
     produced = jnp.dot(shards, moved_weight, preferred_element_type=jnp.float32).astype(
         jnp.bfloat16

time: 366 us -> 590 us (1.61)
  the two profiles are of different devices: /device:TPU:2 before, /device:TPU:56 now
where the time goes in v1:
time: 590 us; the launch traced here: 589 us
  waiting for transfers between devices  461 us (78%)
  starting transfers between devices  50.1 us (8%)
  local copies, waits for them, and re-layouts  26.3 us (4%)
  between operations  16.1 us (3%)
  blocking collectives  15.3 us (3%)
  matrix products  13.6 us (2%)
  other arithmetic  6.51 us (1%)
    all_to_all x1, waiting for transfers between devices, exchange_gather(): blocks = lax.all_to_all(blocks, axis, split_axis=0, concat_axis=0)  363 us
    all_to_all x1, waiting for transfers between devices, local(): lax.all_to_all(output_columns, 'dp', split_axis=0, concat_axis=1, tiled=T...  47.2 us
    all_to_all x1, waiting for transfers between devices, local(): lax.all_to_all(out_grad[0], 'dp', split_axis=1, concat_axis=0, tiled=True)  31.4 us
    all_to_all x1, starting transfers between devices, exchange_gather(): blocks = lax.all_to_all(blocks, axis, split_axis=0, concat_axis=0)  17.9 us
    all_to_all x1, blocking collectives, local(): lax.all_to_all(second_moment[0], 'expert', split_axis=0, concat_axis=0, t...  15.3 us
    all_to_all x1, local copies, waits for them, and re-layouts, exchange_gather(): blocks = lax.all_to_all(blocks, axis, split_axis=0, concat_axis=0)  11.9 us
  transfers between devices with their start and end apart: 7, of which 6 were waited for; matrix products, arithmetic and copies ran while one was open for 7% of the time, Pallas kernels for 0%

profile of v1, /device:TPU:56, one launch (start us, length us, event | category | flops | bytes accessed | tf_op | source)
XLA Modules:
  0.0 589.0 jit_solution(15483867930072437571)
XLA Ops:
  7.2 15.3 %all_to_all.67 = f32[16,64,128]{2,1,0:T(8,128)S(1)} all-to-all(f32[16,64,128]{2,1,0:T(8,128)} %bitcast.41), channel_id=1, replica_groups=mesh['dp'=32,'expert'=16] {'expert'}, dimensions={0} | all-to-all | bytes 1048576 | tf_op jit(solution)/shard_map/all_to_all | solution.py:48
  22.4 4.9 all-to-all-start.2
  28.1 1.4 gather_fusion.1
  29.5 7.3 %all-to-all-done.2 = f32[16,64,128]{2,1,0:T(8,128)S(1)} async-done(((f32[16,64,128]{2,1,0:T(8,128)}), f32[16,64,128]{2,1,0:T(8,128)S(1)}, u32[]{:S(2)}, u32[]{:S(2)}) %all-to-all-start.2) | async-done | bytes 524320 | tf_op jit(solution)/shard_map/all_to_all | solution.py:47
  36.8 4.9 all-to-all-start.6
  41.7 1.4 gather_fusion
  43.1 8.1 %all-to-all-done.6 = f32[16,64,128]{2,1,0:T(8,128)S(1)} async-done(((f32[16,64,128]{2,1,0:T(8,128)}), f32[16,64,128]{2,1,0:T(8,128)S(1)}, u32[]{:S(2)}, u32[]{:S(2)}) %all-to-all-start.6) | async-done | bytes 524320 | tf_op jit(solution)/shard_map/all_to_all | solution.py:52
  51.2 4.9 all-to-all-start.3
  58.7 1.3 dynamic_slice.11
  60.6 1.2 fusion.8
  62.0 3.6 all-to-all-done.3
  65.6 5.1 stack.5
  70.7 17.9 %all-to-all-start = ((bf16[32,128,1024]{1,2,0:T(8,128)(2,1)}), bf16[32,128,1024]{1,2,0:T(8,128)(2,1)}, u32[]{:S(2)}, u32[]{:S(2)}) async-start(bf16[32,128,1024]{1,2,0:T(8,128)(2,1)} %stack.5), calls=%async_computation | async-start | bytes 16777216 | tf_op jit(solution)/shard_map/all_to_all | solution.py:17
  90.1 1.3 copy.29
  91.4 362.7 %all-to-all-done = bf16[32,128,1024]{1,2,0:T(8,128)(2,1)} async-done(((bf16[32,128,1024]{1,2,0:T(8,128)(2,1)}), bf16[32,128,1024]{1,2,0:T(8,128)(2,1)}, u32[]{:S(2)}, u32[]{:S(2)}) %all-to-all-start) | async-done | bytes 8388640 | tf_op jit(solution)/shard_map/all_to_all | solution.py:17
  454.1 11.3 %all-to-all-start.4 = ((bf16[128,32,128]{2,0,1:T(8,128)(2,1)}), bf16[128,32,128]{2,0,1:T(8,128)(2,1)S(1)}, u32[]{:S(2)}, u32[]{:S(2)}) async-start(bf16[128,32,128]{2,0,1:T(8,128)(2,1)} %copy.29), calls=%async_computation.4 | async-start | bytes 2097152 | tf_op jit(solution)/shard_map/all_to_all | solution.py:59
  466.7 3.1 select_reduce_fusion
  469.8 11.9 %copy.26 = bf16[32,128,1024]{2,1,0:T(8,128)(2,1)} copy(bf16[32,128,1024]{1,2,0:T(8,128)(2,1)} %all-to-all-done) | data formatting | bytes 16777216 | tf_op jit(solution)/shard_map/all_to_all | solution.py:17
  481.7 6.7 %convolution_convert_fusion = bf16[4096,128]{1,0:T(8,128)(2,1)} fusion(bf16[4096,1024]{1,0:T(8,128)(2,1)} %bitcast.37, bf16[1024,128]{1,0:T(8,128)(2,1)S(1)} %select_reduce_fusion), kind=kOutput, calls=%fused_computation.2 | convolution fusion | flops 1074266112 | bytes 9699328 | tf_op jit(solution)/shard_map/dot_general | solution.py:62
  488.4 31.4 %all-to-all-done.4 = bf16[128,32,128]{2,0,1:T(8,128)(2,1)S(1)} async-done(((bf16[128,32,128]{2,0,1:T(8,128)(2,1)}), bf16[128,32,128]{2,0,1:T(8,128)(2,1)S(1)}, u32[]{:S(2)}, u32[]{:S(2)}) %all-to-all-start.4) | async-done | bytes 1048608 | tf_op jit(solution)/shard_map/all_to_all | solution.py:59
  519.8 6.1 %all-to-all-start.1 = ((bf16[32,128,128]{2,1,0:T(8,128)(2,1)}), bf16[32,128,128]{2,1,0:T(8,128)(2,1)S(1)}, u32[]{:S(2)}, u32[]{:S(2)}) async-start(bf16[32,128,128]{2,1,0:T(8,128)(2,1)} %bitcast.40), calls=%async_computation.1 | async-start | bytes 2097152 | tf_op jit(solution)/shard_map/all_to_all | solution.py:67
  526.1 6.9 %fusion.9 = (bf16[1,1024,128]{2,1,0:T(8,128)(2,1)}, f32[1024,128]{1,0:T(8,128)}, f32[1024,128]{1,0:T(8,128)}) fusion(bf16[1024,128]{1,0:T(8,128)(2,1)S(1)} %select_reduce_fusion, f32[16,64,128]{2,1,0:T(8,128)S(1)} %broadcast_multiply_fusion.1, f32[16,64,128]{2,1,0:T(8,128)S(1)} %broadcast_multiply_fusion, bf16[32,128,1024]{1,2,0:T(8,128)(2,1)} %all-to-all-done, ...), kind=kOutput, calls=%fused_computation.21 | convolution fusion | flops 1075314688 | bytes 12058624 | tf_op jit(solution)/shard_map/rf,rc->fc/dot_general | solution.py:61
  533.0 47.2 %all-to-all-done.1 = bf16[32,128,128]{2,1,0:T(8,128)(2,1)S(1)} async-done(((bf16[32,128,128]{2,1,0:T(8,128)(2,1)}), bf16[32,128,128]{2,1,0:T(8,128)(2,1)S(1)}, u32[]{:S(2)}, u32[]{:S(2)}) %all-to-all-start.1) | async-done | bytes 1048608 | tf_op jit(solution)/shard_map/all_to_all | solution.py:67
  580.9 1.3 broadcast_in_dim.68
  (17 shorter events, 5.6 us)
Async XLA Ops:
  22.4 14.4 %all-to-all-start.2 = ((f32[16,64,128]{2,1,0:T(8,128)}), f32[16,64,128]{2,1,0:T(8,128)S(1)}, u32[]{:S(2)}, u32[]{:S(2)}) async-start(f32[16,64,128]{2,1,0:T(8,128)} %bitcast.42), calls=%async_computation.2 | async-start | bytes 1048576 | tf_op jit(solution)/shard_map/all_to_all | solution.py:47
  36.8 14.4 %all-to-all-start.6 = ((f32[16,64,128]{2,1,0:T(8,128)}), f32[16,64,128]{2,1,0:T(8,128)S(1)}, u32[]{:S(2)}, u32[]{:S(2)}) async-start(f32[16,64,128]{2,1,0:T(8,128)} %gather_fusion.1), calls=%async_computation.6 | async-start | bytes 1048576 | tf_op jit(solution)/shard_map/all_to_all | solution.py:52
  51.2 14.4 %all-to-all-start.3 = ((f32[16,64,128]{2,1,0:T(8,128)}), f32[16,64,128]{2,1,0:T(8,128)S(1)}, u32[]{:S(2)}, u32[]{:S(2)}) async-start(f32[16,64,128]{2,1,0:T(8,128)} %gather_fusion), calls=%async_computation.3 | async-start | bytes 1048576 | tf_op jit(solution)/shard_map/all_to_all | solution.py:51
  70.7 18.7 %copy-start = (bf16[1,128,4096]{2,1,0:T(8,128)(2,1)S(1)}, bf16[1,128,4096]{2,1,0:T(8,128)(2,1)}, u32[]{:S(2)}) copy-start(bf16[1,128,4096]{2,1,0:T(8,128)(2,1)} %param.14) | copy-start | bytes 3145732
  70.7 383.4 %all-to-all-start = ((bf16[32,128,1024]{1,2,0:T(8,128)(2,1)}), bf16[32,128,1024]{1,2,0:T(8,128)(2,1)}, u32[]{:S(2)}, u32[]{:S(2)}) async-start(bf16[32,128,1024]{1,2,0:T(8,128)(2,1)} %stack.5), calls=%async_computation | async-start | bytes 16777216 | tf_op jit(solution)/shard_map/all_to_all | solution.py:17
  88.7 378.0 %all-gather.2.cloned.1.call-start = ((), (), s32[]{:S(2)}) async-start(), calls=%async_computation.7 | async-start | bytes 4456448 | tf_op jit(solution)/shard_map/all_gather | solution.py:43
  454.1 65.7 %all-to-all-start.4 = ((bf16[128,32,128]{2,0,1:T(8,128)(2,1)}), bf16[128,32,128]{2,0,1:T(8,128)(2,1)S(1)}, u32[]{:S(2)}, u32[]{:S(2)}) async-start(bf16[128,32,128]{2,0,1:T(8,128)(2,1)} %copy.29), calls=%async_computation.4 | async-start | bytes 2097152 | tf_op jit(solution)/shard_map/all_to_all | solution.py:59
  519.8 60.4 %all-to-all-start.1 = ((bf16[32,128,128]{2,1,0:T(8,128)(2,1)}), bf16[32,128,128]{2,1,0:T(8,128)(2,1)S(1)}, u32[]{:S(2)}, u32[]{:S(2)}) async-start(bf16[32,128,128]{2,1,0:T(8,128)(2,1)} %bitcast.40), calls=%async_computation.1 | async-start | bytes 2097152 | tf_op jit(solution)/shard_map/all_to_all | solution.py:67
Sparse Core Ops, SparseCore 0:
  91.7 45.7 all-gather.1
